TPU v7x, 32 devices: a whole 2x2x4 slice. The times are simulated.
32 devices in a mesh: seq: 16 (over z, x, core), head: 2 (over y).
Axes of the slice: x: 2, y: 2, z: 4, core: 2. Of those that a mesh axis runs over, the one named last changes fastest.
Arguments:
- queries: bfloat16 [8192, 3072], P(('seq', 'head'))
- keys: bfloat16 [8192, 3072], P(('seq', 'head'))
- values: bfloat16 [8192, 3072], P(('seq', 'head')), may hold values from -6 to 6
- kv_blocks: int32 [64, 64], replicated, may hold values from 0 to 63, as said below
- block_counts: int32 [64, 16], replicated, may hold values from 0 to 4, as said below
Outputs:
- attended: bfloat16 [8192, 3072], P(('seq', 'head'))
Inputs may be any that keep to these rules, and one draw needn't show every extreme that they name: `kv_blocks`: slot f * 4 + j names a key block of frame f, as a global block index f * 4 + local; the valid slots of one query block and frame name distinct blocks; slots at or beyond block_counts carry a block of the same frame and no meaning. With e the distance between frame f and the frame of query block b: block_counts[b, f] is 4 where e is 0, at most 2 where e is 1, at most 1 where e is 2, 3 or a power of two, and 0 otherwise; each of these largest values is taken by the first query block of every frame.
All inputs are finite; a program needn't handle non-finite values.
Results may differ from a plain program's by a relative error of at most 0.02.
Values may be sent and summed in bfloat16 or wider, within the bound.
A program may use at most 128 MiB of HBM per device.

v0:
```python
import jax
import jax.numpy as jnp
from jax import lax
from jax.sharding import PartitionSpec as P

HD = 128
BLK = 128
SLOTS = 4
NEG_FILL = -1e30


def from_behind(block, axis, distance):
    devices = range(lax.axis_size(axis))
    route = [(i - distance, i) for i in devices if i - distance in devices]
    return lax.ppermute(block, axis, route)


def rotate_time(matrix, frame_ids):
    row_count = matrix.shape[0]
    head_count = matrix.shape[1] // HD
    per_head = matrix.reshape(row_count, head_count, HD)
    pair_index = jnp.arange(8, dtype=jnp.float32)
    frequency = 256.0 ** (-pair_index / 8.0)
    angles = frame_ids.astype(jnp.float32)[:, None] * frequency[None, :]
    cosine = jnp.cos(angles)[:, None, :]
    sine_part = jnp.sin(angles)[:, None, :]
    pair_view = per_head[:, :, :16].reshape(row_count, head_count, 8, 2)
    even_part = pair_view[..., 0]
    odd_part = pair_view[..., 1]
    turned = jnp.stack(
        [even_part * cosine - odd_part * sine_part, even_part * sine_part + odd_part * cosine],
        axis=-1,
    )
    joined = jnp.concatenate(
        [turned.reshape(row_count, head_count, 16), per_head[:, :, 16:]], axis=2
    )
    return joined.reshape(row_count, head_count * HD)


def signed_distances(frame_count):
    base = [1, 2, 3]
    power = 4
    while power < frame_count:
        base.append(power)
        power = power * 2
    result = [0]
    for step in base:
        result.append(step)
        result.append(-step)
    return result


def slot_cap(distance):
    if distance == 0:
        return SLOTS
    if abs(distance) == 1:
        return 2
    return 1


def block_table(kv_blocks, block_counts, query_frame, key_frame, cap, frame_blocks, frame_count):
    valid = (
        (query_frame >= 0)
        & (query_frame < frame_count)
        & (key_frame >= 0)
        & (key_frame < frame_count)
    )
    query_clip = jnp.clip(query_frame, 0, frame_count - 1)
    key_clip = jnp.clip(key_frame, 0, frame_count - 1)
    row_start = query_clip * frame_blocks
    block_ids = (
        lax.dynamic_slice(kv_blocks, (row_start, key_clip * SLOTS), (frame_blocks, cap))
        - key_clip * frame_blocks
    )
    counts = lax.dynamic_slice(block_counts, (row_start, key_clip), (frame_blocks, 1))[:, 0]
    return (block_ids, jnp.where(valid, counts, 0), valid)


def frame_partial(query_group, key_blocks, value_blocks, block_ids, valid_counts, cap):
    picked_keys = key_blocks[block_ids]
    picked_values = value_blocks[block_ids]
    scores = jnp.einsum(
        "bqhd,bskhd->bhqsk", query_group, picked_keys, preferred_element_type=jnp.float32
    ) * HD ** (-0.5)
    usable = (jnp.arange(cap, dtype=jnp.int32)[None, :] < valid_counts[:, None])[
        :, None, None, :, None
    ]
    masked = jnp.where(usable, scores, NEG_FILL)
    part_max = jnp.max(masked, axis=(3, 4))
    probs = jnp.where(usable, jnp.exp(masked - part_max[..., None, None]), 0.0)
    part_sum = jnp.sum(probs, axis=(3, 4))
    part_num = jnp.einsum(
        "bhqsk,bskhd->bqhd",
        probs.astype(jnp.bfloat16),
        picked_values,
        preferred_element_type=jnp.float32,
    )
    return (part_num.astype(jnp.bfloat16), part_max, part_sum)


def guarded_partial(query_group, key_blocks, value_blocks, block_ids, valid_counts, cap):
    return frame_partial(query_group, key_blocks, value_blocks, block_ids, valid_counts, cap)


def merge_state(state, part):
    run_max, run_sum, run_num = state
    part_num, part_max, part_sum = part
    new_max = jnp.maximum(run_max, part_max)
    old_scale = jnp.exp(run_max - new_max)
    new_scale = jnp.exp(part_max - new_max)
    run_sum = old_scale * run_sum + new_scale * part_sum
    run_num = (
        run_num * jnp.transpose(old_scale, (0, 2, 1))[..., None]
        + part_num.astype(jnp.float32) * jnp.transpose(new_scale, (0, 2, 1))[..., None]
    )
    return (new_max, run_sum, run_num)


def local(queries, keys, values, kv_blocks, block_counts):
    seq_index = lax.axis_index("seq")
    frame_count = lax.axis_size("seq")
    query_slab = lax.all_to_all(queries, "head", split_axis=1, concat_axis=0, tiled=True)
    key_slab, value_slab = (
        lax.all_to_all(keys, "head", split_axis=1, concat_axis=0, tiled=True),
        lax.all_to_all(values, "head", split_axis=1, concat_axis=0, tiled=True),
    )
    frame_tokens = key_slab.shape[0]
    row_width = key_slab.shape[1]
    head_count = row_width // HD
    frame_blocks = frame_tokens // BLK
    frame_ids = jnp.zeros((frame_tokens,), jnp.int32) + seq_index
    query_turned = rotate_time(query_slab.astype(jnp.float32), frame_ids).astype(jnp.bfloat16)
    key_turned = rotate_time(key_slab.astype(jnp.float32), frame_ids).astype(jnp.bfloat16)
    query_group = query_turned.reshape(frame_blocks, BLK, head_count, HD)
    key_blocks = key_turned.reshape(frame_blocks, BLK, head_count, HD)
    value_blocks = value_slab.reshape(frame_blocks, BLK, head_count, HD)
    stat_shape = (frame_blocks, head_count, BLK)
    state = (
        jnp.full(stat_shape, NEG_FILL, jnp.float32),
        jnp.zeros(stat_shape, jnp.float32),
        jnp.zeros((frame_blocks, BLK, head_count, HD), jnp.float32),
    )
    for distance in signed_distances(frame_count):
        cap = slot_cap(distance)
        if distance == 0:
            block_ids, counts, valid = block_table(
                kv_blocks, block_counts, seq_index, seq_index, cap, frame_blocks, frame_count
            )
            part = frame_partial(query_group, key_blocks, value_blocks, block_ids, counts, cap)
        else:
            far_keys, far_values = from_behind((key_blocks, value_blocks), "seq", distance)
            block_ids, counts, valid = block_table(
                kv_blocks,
                block_counts,
                seq_index,
                seq_index - distance,
                cap,
                frame_blocks,
                frame_count,
            )
            part = guarded_partial(query_group, far_keys, far_values, block_ids, counts, cap)
        state = merge_state(state, part)
    denominator = jnp.transpose(state[1], (0, 2, 1))[..., None]
    attended = (state[2] / denominator).reshape(frame_tokens, row_width).astype(jnp.bfloat16)
    return lax.all_to_all(attended, "head", split_axis=0, concat_axis=1, tiled=True)


def solution(mesh):
    in_specs = (
        P(("seq", "head"), None),
        P(("seq", "head"), None),
        P(("seq", "head"), None),
        P(),
        P(),
    )
    out_specs = P(("seq", "head"), None)
    return jax.shard_map(local, mesh=mesh, in_specs=in_specs, out_specs=out_specs, check_vma=False)
```

profile of v0, /device:TPU:26, one launch (start us, length us, event | category | flops | bytes accessed | tf_op | source)
XLA Modules:
  0.0 654.6 jit_solution(9133775101212698396)
XLA Ops:
  9.5 16.3 %all-to-all-done.1 = bf16[256,2,1536]{0,2,1:T(8,128)(2,1)S(1)} async-done(((bf16[256,2,1536]{0,2,1:T(8,128)(2,1)}), bf16[256,2,1536]{0,2,1:T(8,128)(2,1)S(1)}, u32[]{:S(2)}, u32[]{:S(2)}) %all-to-all-start.1) | async-done | bytes 1572896 | tf_op jit(solution)/shard_map/all_to_all | solution.py:124
  35.6 12.6 %all-to-all-done.2 = bf16[256,2,1536]{0,2,1:T(8,128)(2,1)S(1)} async-done(((bf16[256,2,1536]{0,2,1:T(8,128)(2,1)}), bf16[256,2,1536]{0,2,1:T(8,128)(2,1)S(1)}, u32[]{:S(2)}, u32[]{:S(2)}) %all-to-all-start.2) | async-done | bytes 1572896 | tf_op jit(solution)/shard_map/all_to_all | solution.py:125
  48.1 4.6 all-to-all-start
  54.6 10.7 %copy.203 = bf16[2,256,1536]{1,0,2:T(2,128)(2,1)} copy(bf16[2,256,1536]{1,2,0:T(8,128)(2,1)S(1)} %bitcast.448) | data formatting | bytes 3145728 | tf_op jit(solution)/shard_map/all_to_all | solution.py:125
  65.3 5.2 reshape.374
  79.4 10.7 %copy.195 = bf16[2,256,1536]{1,0,2:T(2,128)(2,1)} copy(bf16[2,256,1536]{1,2,0:T(8,128)(2,1)S(1)} %bitcast.447) | data formatting | bytes 3145728 | tf_op jit(solution)/shard_map/convert_element_type | solution.py:133
  94.1 4.8 copy.188
  125.8 6.1 collective-permute-start.10
  140.0 5.5 gather_fusion
  152.2 4.3 copy.201
  157.4 5.6 fusion
  163.1 5.7 collective-permute-start.7
  170.1 9.9 %collective-permute-done.12 = bf16[4,128,12,128]{3,1,2,0:T(8,128)(2,1)} collective-permute-done((bf16[4,128,12,128]{3,1,2,0:T(8,128)(2,1)}, bf16[4,128,12,128]{3,1,2,0:T(8,128)(2,1)}, u32[]{:S(2)}, u32[]{:S(2)}) %collective-permute-start.12) | collective-permute-done | bytes 1572896 | tf_op jit(solution)/shard_map/ppermute | solution.py:15
  183.7 11.9 %bitcast_convert_fusion.2 = bf16[4,12,128,128]{3,2,1,0:T(8,128)(2,1)} fusion(f32[4,12,128,512]{2,3,1,0} %get-tuple-element.88, f32[4,12,128]{2,1,0:T(8,128)S(1)} %get-tuple-element.87, pred[4,4]{1,0:T(4,128)(4,1)S(1)} %copy-done.73, bf16[4,4,128,12,128]{4,2,3,1,0:T(8,128)(2,1)} %bitcast.446), kind=kOutput, calls=%fused_computation.84 | convolution fusion | flops 821821440 | bytes 20471824 | tf_op jit(solution)/shard_map/bhqsk,bskhd->bqhd/dot_general | solution.py:92
  195.5 12.2 %collective-permute-done.8 = bf16[4,128,12,128]{3,1,2,0:T(8,128)(2,1)} collective-permute-done((bf16[4,128,12,128]{3,1,2,0:T(8,128)(2,1)}, bf16[4,128,12,128]{3,1,2,0:T(8,128)(2,1)}, u32[]{:S(2)}, u32[]{:S(2)}) %collective-permute-start.8) | collective-permute-done | bytes 1572896 | tf_op jit(solution)/shard_map/ppermute | solution.py:15
  209.2 6.6 %fusion.1 = f32[4,12,128]{2,1,0:T(8,128)S(1)} fusion(f32[4,12,128,512]{2,3,1,0} %get-tuple-element.88, f32[4,12,128]{2,1,0:T(8,128)S(1)} %get-tuple-element.87, pred[4,4]{1,0:T(4,128)(4,1)S(1)} %copy-done.73), kind=kLoop, calls=%fused_computation.25 | loop fusion | flops 15722496 | bytes 12632080 | tf_op jit(solution)/shard_map/reduce_sum | solution.py:91
  236.3 48.8 %collective-permute-done.7 = bf16[4,128,12,128]{3,1,2,0:T(8,128)(2,1)} collective-permute-done((bf16[4,128,12,128]{3,1,2,0:T(8,128)(2,1)S(1)}, bf16[4,128,12,128]{3,1,2,0:T(8,128)(2,1)}, u32[]{:S(2)}, u32[]{:S(2)}) %collective-permute-start.7) | collective-permute-done | bytes 1572896 | tf_op jit(solution)/shard_map/ppermute | solution.py:15
  285.2 9.1 %collective-permute-start.19 = (bf16[4,128,12,128]{3,1,2,0:T(8,128)(2,1)S(1)}, bf16[4,128,12,128]{3,1,2,0:T(8,128)(2,1)}, u32[]{:S(2)}, u32[]{:S(2)}) collective-permute-start(bf16[4,128,12,128]{3,1,2,0:T(8,128)(2,1)S(1)} %copy.204), channel_id=1, source_target_pairs={{16,0},{18,2},{20,4},{22,6},{24,8},{26,10},{28,12},{30,14},{17,1},... | collective-permute-start | bytes 4718600 | tf_op jit(solution)/shard_map/ppermute | solution.py:15
  297.6 21.3 %collective-permute-done.6 = bf16[4,128,12,128]{3,1,2,0:T(8,128)(2,1)} collective-permute-done((bf16[4,128,12,128]{3,1,2,0:T(8,128)(2,1)}, bf16[4,128,12,128]{3,1,2,0:T(8,128)(2,1)}, u32[]{:S(2)}, u32[]{:S(2)}) %collective-permute-start.6) | collective-permute-done | bytes 1572896 | tf_op jit(solution)/shard_map/ppermute | solution.py:15
  319.0 7.5 %collective-permute-start.15 = (bf16[4,128,12,128]{3,1,2,0:T(8,128)(2,1)S(1)}, bf16[4,128,12,128]{3,1,2,0:T(8,128)(2,1)}, u32[]{:S(2)}, u32[]{:S(2)}) collective-permute-start(bf16[4,128,12,128]{3,1,2,0:T(8,128)(2,1)S(1)} %copy.204), channel_id=1, source_target_pairs={{8,0},{10,2},{12,4},{14,6},{16,8},{18,10},{20,12},{22,14},{24,16},... | collective-permute-start | bytes 4718600 | tf_op jit(solution)/shard_map/ppermute | solution.py:15
  341.7 4.4 fusion.56
  361.0 4.4 fusion.60
  373.5 52.1 %collective-permute-done.14 = bf16[4,128,12,128]{3,1,2,0:T(8,128)(2,1)} collective-permute-done((bf16[4,128,12,128]{3,1,2,0:T(8,128)(2,1)}, bf16[4,128,12,128]{3,1,2,0:T(8,128)(2,1)}, u32[]{:S(2)}, u32[]{:S(2)}) %collective-permute-start.14) | collective-permute-done | bytes 1572896 | tf_op jit(solution)/shard_map/ppermute | solution.py:15
  431.4 4.4 fusion.61
  476.0 5.2 fusion.13
  489.0 4.3 convolution_convert_fusion.2
  498.9 82.6 %collective-permute-done.17 = bf16[4,128,12,128]{3,1,2,0:T(8,128)(2,1)} collective-permute-done((bf16[4,128,12,128]{3,1,2,0:T(8,128)(2,1)S(1)}, bf16[4,128,12,128]{3,1,2,0:T(8,128)(2,1)}, u32[]{:S(2)}, u32[]{:S(2)}) %collective-permute-start.17) | collective-permute-done | bytes 1572896 | tf_op jit(solution)/shard_map/ppermute | solution.py:15
  584.0 4.3 convolution_convert_fusion.1
  599.3 4.1 gather_fusion.3
  603.4 7.2 %bitcast_convert_fusion.1 = bf16[4,12,128,128]{3,2,1,0:T(8,128)(2,1)} fusion(f32[4,12,128,256]{2,3,1,0} %get-tuple-element.86, f32[4,12,128]{2,1,0:T(8,128)S(1)} %get-tuple-element.85, pred[4,2]{1,0:T(4,128)(4,1)S(1)} %copy-done.54, bf16[4,2,128,12,128]{4,2,3,1,0:T(8,128)(2,1)} %bitcast.453), kind=kOutput, calls=%fused_computation.79 | convolution fusion | flops 411303936 | bytes 11034632 | tf_op jit(solution)/shard_map/bhqsk,bskhd->bqhd/dot_general | solution.py:92
  617.6 9.7 %fusion.23 = bf16[4,128,12,128]{1,3,2,0:T(8,128)(2,1)S(1)} fusion(bf16[4,12,128,128]{3,2,1,0:T(8,128)(2,1)} %convolution_convert_fusion.1, bf16[4,12,128,128]{3,2,1,0:T(8,128)(2,1)} %convolution_convert_fusion.2, bf16[4,12,128,128]{3,2,1,0:T(8,128)(2,1)} %convolution_convert_fusion.3, bf16[4,12,128,128]{3,2,1,0:T(8,128)(2,1)} %convolution_convert_fusion.4, ...), kind=kOutput, calls=%fused_computation.49 | convolution fusion | flops 241434624 | bytes 22609924 | tf_op jit(solution)/shard_map/bhqsk,bskhd->bqhd/dot_general | solution.py:92
  629.9 22.8 %all_to_all.58 = bf16[2,256,1536]{1,2,0:T(8,128)(2,1)S(1)} all-to-all(bf16[2,256,1536]{1,2,0:T(8,128)(2,1)S(1)} %copy.248), channel_id=1, replica_groups=mesh['seq'=16,'head'=2] {'head'}, dimensions={0} | all-to-all | bytes 3145728 | tf_op jit(solution)/shard_map/all_to_all | solution.py:165
  (300 shorter events, 228.4 us)
Async XLA Ops:
  0.0 7.4 %copy-start.31 = (bf16[256,3072]{1,0:T(8,128)(2,1)S(1)}, bf16[256,3072]{1,0:T(8,128)(2,1)}, u32[]{:S(2)}) copy-start(bf16[256,3072]{1,0:T(8,128)(2,1)} %param.7) | copy-start | bytes 4718596
  2.7 23.2 %all-to-all-start.1 = ((bf16[256,2,1536]{0,2,1:T(8,128)(2,1)}), bf16[256,2,1536]{0,2,1:T(8,128)(2,1)S(1)}, u32[]{:S(2)}, u32[]{:S(2)}) async-start(bf16[256,2,1536]{0,2,1:T(8,128)(2,1)} %bitcast.3), calls=%async_computation.1 | async-start | bytes 3145728 | tf_op jit(solution)/shard_map/all_to_all | solution.py:124
  25.9 22.3 %all-to-all-start.2 = ((bf16[256,2,1536]{0,2,1:T(8,128)(2,1)}), bf16[256,2,1536]{0,2,1:T(8,128)(2,1)S(1)}, u32[]{:S(2)}, u32[]{:S(2)}) async-start(bf16[256,2,1536]{0,2,1:T(8,128)(2,1)} %bitcast.449), calls=%async_computation.2 | async-start | bytes 3145728 | tf_op jit(solution)/shard_map/all_to_all | solution.py:125
  48.1 46.0 %all-to-all-start = ((bf16[256,2,1536]{0,2,1:T(8,128)(2,1)}), bf16[256,2,1536]{0,2,1:T(8,128)(2,1)}, u32[]{:S(2)}, u32[]{:S(2)}) async-start(bf16[256,2,1536]{0,2,1:T(8,128)(2,1)} %bitcast.450), calls=%async_computation | async-start | bytes 3145728 | tf_op jit(solution)/shard_map/all_to_all | solution.py:122
  73.2 61.3 %collective-permute-start.13 = (bf16[4,128,12,128]{3,1,2,0:T(8,128)(2,1)S(1)}, bf16[4,128,12,128]{3,1,2,0:T(8,128)(2,1)}, u32[]{:S(2)}, u32[]{:S(2)}) collective-permute-start(bf16[4,128,12,128]{3,1,2,0:T(8,128)(2,1)S(1)} %copy.204), channel_id=1, source_target_pairs={{0,8},{2,10},{4,12},{6,14},{8,16},{10,18},{12,20},{14,22},{16,24},... | collective-permute-start | bytes 4718600 | tf_op jit(solution)/shard_map/ppermute | solution.py:15
  74.5 88.6 %collective-permute-start.11 = (bf16[4,128,12,128]{3,1,2,0:T(8,128)(2,1)S(1)}, bf16[4,128,12,128]{3,1,2,0:T(8,128)(2,1)}, u32[]{:S(2)}, u32[]{:S(2)}) collective-permute-start(bf16[4,128,12,128]{3,1,2,0:T(8,128)(2,1)S(1)} %copy.204), channel_id=1, source_target_pairs={{6,0},{8,2},{10,4},{12,6},{14,8},{16,10},{18,12},{20,14},{22,16},{... | collective-permute-start | bytes 4718600 | tf_op jit(solution)/shard_map/ppermute | solution.py:15
  77.6 91.2 %collective-permute-start.9 = (bf16[4,128,12,128]{3,1,2,0:T(8,128)(2,1)S(1)}, bf16[4,128,12,128]{3,1,2,0:T(8,128)(2,1)}, u32[]{:S(2)}, u32[]{:S(2)}) collective-permute-start(bf16[4,128,12,128]{3,1,2,0:T(8,128)(2,1)S(1)} %copy.204), channel_id=1, source_target_pairs={{0,6},{2,8},{4,10},{6,12},{8,14},{10,16},{12,18},{14,20},{16,22},{... | collective-permute-start | bytes 4718600 | tf_op jit(solution)/shard_map/ppermute | solution.py:15
  101.8 34.2 %copy-start.22 = (bf16[512,12,128]{0,2,1:T(8,128)(2,1)}, bf16[512,12,128]{0,2,1:T(8,128)(2,1)S(1)}, u32[]{:S(2)}) copy-start(bf16[512,12,128]{0,2,1:T(8,128)(2,1)S(1)} %convert_element_type.184) | copy-start | bytes 4718596
  119.0 13.6 %copy-start.74 = (s32[4,1]{0,1:T(1,128)S(1)}, s32[4,1]{0,1:T(1,128)}, u32[]{:S(2)}) copy-start(s32[4,1]{0,1:T(1,128)} %copy.289) | copy-start | bytes 52
  119.0 17.0 %copy-start.32 = (bf16[512,12,8,1]{0,2,3,1:T(8,128)(2,1)S(1)}, bf16[512,12,8,1]{0,2,3,1:T(8,128)(2,1)}, u32[]{:S(2)}) copy-start(bf16[512,12,8,1]{0,2,3,1:T(8,128)(2,1)} %get-tuple-element.67) | copy-start | bytes 294916
  119.0 17.0 %copy-start.33 = (bf16[512,12,8,1]{0,2,3,1:T(8,128)(2,1)S(1)}, bf16[512,12,8,1]{0,2,3,1:T(8,128)(2,1)}, u32[]{:S(2)}) copy-start(bf16[512,12,8,1]{0,2,3,1:T(8,128)(2,1)} %get-tuple-element.68) | copy-start | bytes 294916
  120.5 11.4 %copy-start.72 = (s32[64,16]{0,1:T(8,128)S(1)}, s32[64,16]{0,1:T(8,128)}, u32[]{:S(2)}) copy-start(s32[64,16]{0,1:T(8,128)} %param.9) | copy-start | bytes 12292
  120.5 11.4 %copy-start.75 = (s32[4,1]{0,1:T(1,128)S(1)}, s32[4,1]{0,1:T(1,128)}, u32[]{:S(2)}) copy-start(s32[4,1]{0,1:T(1,128)} %copy.288) | copy-start | bytes 52
  124.5 55.5 %collective-permute-start.12 = (bf16[4,128,12,128]{3,1,2,0:T(8,128)(2,1)}, bf16[4,128,12,128]{3,1,2,0:T(8,128)(2,1)}, u32[]{:S(2)}, u32[]{:S(2)}) collective-permute-start(bf16[4,128,12,128]{3,1,2,0:T(8,128)(2,1)} %pad_maximum_fusion.1), channel_id=1, source_target_pairs={{0,8},{2,10},{4,12},{6,14},{8,16},{10,18},{12,20},{14,22},{16,24},... | collective-permute-start | bytes 4718600 | tf_op jit(solution)/shard_map/ppermute | solution.py:15
  125.8 56.6 %collective-permute-start.10 = (bf16[4,128,12,128]{3,1,2,0:T(8,128)(2,1)}, bf16[4,128,12,128]{3,1,2,0:T(8,128)(2,1)}, u32[]{:S(2)}, u32[]{:S(2)}) collective-permute-start(bf16[4,128,12,128]{3,1,2,0:T(8,128)(2,1)} %pad_maximum_fusion.1), channel_id=1, source_target_pairs={{6,0},{8,2},{10,4},{12,6},{14,8},{16,10},{18,12},{20,14},{22,16},{... | collective-permute-start | bytes 4718600 | tf_op jit(solution)/shard_map/ppermute | solution.py:15
  134.5 73.2 %collective-permute-start.8 = (bf16[4,128,12,128]{3,1,2,0:T(8,128)(2,1)}, bf16[4,128,12,128]{3,1,2,0:T(8,128)(2,1)}, u32[]{:S(2)}, u32[]{:S(2)}) collective-permute-start(bf16[4,128,12,128]{3,1,2,0:T(8,128)(2,1)} %pad_maximum_fusion.1), channel_id=1, source_target_pairs={{0,6},{2,8},{4,10},{6,12},{8,14},{10,16},{12,18},{14,20},{16,22},{... | collective-permute-start | bytes 4718600 | tf_op jit(solution)/shard_map/ppermute | solution.py:15
  163.1 122.1 %collective-permute-start.7 = (bf16[4,128,12,128]{3,1,2,0:T(8,128)(2,1)S(1)}, bf16[4,128,12,128]{3,1,2,0:T(8,128)(2,1)}, u32[]{:S(2)}, u32[]{:S(2)}) collective-permute-start(bf16[4,128,12,128]{3,1,2,0:T(8,128)(2,1)S(1)} %copy.204), channel_id=1, source_target_pairs={{4,0},{6,2},{8,4},{10,6},{12,8},{14,10},{16,12},{18,14},{20,16},{2... | collective-permute-start | bytes 4718600 | tf_op jit(solution)/shard_map/ppermute | solution.py:15
  168.8 161.1 %collective-permute-start.5 = (bf16[4,128,12,128]{3,1,2,0:T(8,128)(2,1)S(1)}, bf16[4,128,12,128]{3,1,2,0:T(8,128)(2,1)}, u32[]{:S(2)}, u32[]{:S(2)}) collective-permute-start(bf16[4,128,12,128]{3,1,2,0:T(8,128)(2,1)S(1)} %copy.204), channel_id=1, source_target_pairs={{0,4},{2,6},{4,8},{6,10},{8,12},{10,14},{12,16},{14,18},{16,20},{1... | collective-permute-start | bytes 4718600 | tf_op jit(solution)/shard_map/ppermute | solution.py:15
  180.0 139.0 %collective-permute-start.6 = (bf16[4,128,12,128]{3,1,2,0:T(8,128)(2,1)}, bf16[4,128,12,128]{3,1,2,0:T(8,128)(2,1)}, u32[]{:S(2)}, u32[]{:S(2)}) collective-permute-start(bf16[4,128,12,128]{3,1,2,0:T(8,128)(2,1)} %pad_maximum_fusion.1), channel_id=1, source_target_pairs={{4,0},{6,2},{8,4},{10,6},{12,8},{14,10},{16,12},{18,14},{20,16},{2... | collective-permute-start | bytes 4718600 | tf_op jit(solution)/shard_map/ppermute | solution.py:15
  182.4 153.4 %collective-permute-start.4 = (bf16[4,128,12,128]{3,1,2,0:T(8,128)(2,1)}, bf16[4,128,12,128]{3,1,2,0:T(8,128)(2,1)}, u32[]{:S(2)}, u32[]{:S(2)}) collective-permute-start(bf16[4,128,12,128]{3,1,2,0:T(8,128)(2,1)} %pad_maximum_fusion.1), channel_id=1, source_target_pairs={{0,4},{2,6},{4,8},{6,10},{8,12},{10,14},{12,16},{14,18},{16,20},{1... | collective-permute-start | bytes 4718600 | tf_op jit(solution)/shard_map/ppermute | solution.py:15
  207.7 147.3 %collective-permute-start.16 = (bf16[4,128,12,128]{3,1,2,0:T(8,128)(2,1)}, bf16[4,128,12,128]{3,1,2,0:T(8,128)(2,1)}, u32[]{:S(2)}, u32[]{:S(2)}) collective-permute-start(bf16[4,128,12,128]{3,1,2,0:T(8,128)(2,1)} %pad_maximum_fusion.1), channel_id=1, source_target_pairs={{0,16},{2,18},{4,20},{6,22},{8,24},{10,26},{12,28},{14,30},{1,17},... | collective-permute-start | bytes 4718600 | tf_op jit(solution)/shard_map/ppermute | solution.py:15
  285.2 328.9 %collective-permute-start.19 = (bf16[4,128,12,128]{3,1,2,0:T(8,128)(2,1)S(1)}, bf16[4,128,12,128]{3,1,2,0:T(8,128)(2,1)}, u32[]{:S(2)}, u32[]{:S(2)}) collective-permute-start(bf16[4,128,12,128]{3,1,2,0:T(8,128)(2,1)S(1)} %copy.204), channel_id=1, source_target_pairs={{16,0},{18,2},{20,4},{22,6},{24,8},{26,10},{28,12},{30,14},{17,1},... | collective-permute-start | bytes 4718600 | tf_op jit(solution)/shard_map/ppermute | solution.py:15
  319.0 167.6 %collective-permute-start.15 = (bf16[4,128,12,128]{3,1,2,0:T(8,128)(2,1)S(1)}, bf16[4,128,12,128]{3,1,2,0:T(8,128)(2,1)}, u32[]{:S(2)}, u32[]{:S(2)}) collective-permute-start(bf16[4,128,12,128]{3,1,2,0:T(8,128)(2,1)S(1)} %copy.204), channel_id=1, source_target_pairs={{8,0},{10,2},{12,4},{14,6},{16,8},{18,10},{20,12},{22,14},{24,16},... | collective-permute-start | bytes 4718600 | tf_op jit(solution)/shard_map/ppermute | solution.py:15
  329.9 140.7 %collective-permute-start.18 = (bf16[4,128,12,128]{3,1,2,0:T(8,128)(2,1)}, bf16[4,128,12,128]{3,1,2,0:T(8,128)(2,1)}, u32[]{:S(2)}, u32[]{:S(2)}) collective-permute-start(bf16[4,128,12,128]{3,1,2,0:T(8,128)(2,1)} %pad_maximum_fusion.1), channel_id=1, source_target_pairs={{16,0},{18,2},{20,4},{22,6},{24,8},{26,10},{28,12},{30,14},{17,1},... | collective-permute-start | bytes 4718600 | tf_op jit(solution)/shard_map/ppermute | solution.py:15
  335.8 89.8 %collective-permute-start.14 = (bf16[4,128,12,128]{3,1,2,0:T(8,128)(2,1)}, bf16[4,128,12,128]{3,1,2,0:T(8,128)(2,1)}, u32[]{:S(2)}, u32[]{:S(2)}) collective-permute-start(bf16[4,128,12,128]{3,1,2,0:T(8,128)(2,1)} %pad_maximum_fusion.1), channel_id=1, source_target_pairs={{8,0},{10,2},{12,4},{14,6},{16,8},{18,10},{20,12},{22,14},{24,16},... | collective-permute-start | bytes 4718600 | tf_op jit(solution)/shard_map/ppermute | solution.py:15
  355.0 89.0 %collective-permute-start.2 = (bf16[4,128,12,128]{3,1,2,0:T(8,128)(2,1)}, bf16[4,128,12,128]{3,1,2,0:T(8,128)(2,1)}, u32[]{:S(2)}, u32[]{:S(2)}) collective-permute-start(bf16[4,128,12,128]{3,1,2,0:T(8,128)(2,1)} %pad_maximum_fusion.1), channel_id=1, source_target_pairs={{2,0},{4,2},{6,4},{8,6},{10,8},{12,10},{14,12},{16,14},{18,16},{20... | collective-permute-start | bytes 4718600 | tf_op jit(solution)/shard_map/ppermute | solution.py:15
  373.5 57.9 %copy-start.60 = (pred[4]{0:T(512)(128)(4,1)S(1)}, pred[4]{0:T(512)(128)(4,1)}, u32[]{:S(2)}) copy-start(pred[4]{0:T(512)(128)(4,1)} %get-tuple-element.57) | copy-start | bytes 16
  425.7 27.6 %collective-permute-start = (bf16[4,128,12,128]{3,1,2,0:T(8,128)(2,1)}, bf16[4,128,12,128]{3,1,2,0:T(8,128)(2,1)}, u32[]{:S(2)}, u32[]{:S(2)}) collective-permute-start(bf16[4,128,12,128]{3,1,2,0:T(8,128)(2,1)} %pad_maximum_fusion.1), channel_id=1, source_target_pairs={{0,2},{2,4},{4,6},{6,8},{8,10},{10,12},{12,14},{14,16},{16,18},{18... | collective-permute-start | bytes 4718600 | tf_op jit(solution)/shard_map/ppermute | solution.py:15
  444.0 137.6 %collective-permute-start.17 = (bf16[4,128,12,128]{3,1,2,0:T(8,128)(2,1)S(1)}, bf16[4,128,12,128]{3,1,2,0:T(8,128)(2,1)}, u32[]{:S(2)}, u32[]{:S(2)}) collective-permute-start(bf16[4,128,12,128]{3,1,2,0:T(8,128)(2,1)S(1)} %copy.204), channel_id=1, source_target_pairs={{0,16},{2,18},{4,20},{6,22},{8,24},{10,26},{12,28},{14,30},{1,17},... | collective-permute-start | bytes 4718600 | tf_op jit(solution)/shard_map/ppermute | solution.py:15
  453.2 142.0 %collective-permute-start.3 = (bf16[4,128,12,128]{3,1,2,0:T(8,128)(2,1)S(1)}, bf16[4,128,12,128]{3,1,2,0:T(8,128)(2,1)}, u32[]{:S(2)}, u32[]{:S(2)}) collective-permute-start(bf16[4,128,12,128]{3,1,2,0:T(8,128)(2,1)S(1)} %copy.204), channel_id=1, source_target_pairs={{2,0},{4,2},{6,4},{8,6},{10,8},{12,10},{14,12},{16,14},{18,16},{20... | collective-permute-start | bytes 4718600 | tf_op jit(solution)/shard_map/ppermute | solution.py:15
  470.6 128.7 %collective-permute-start.1 = (bf16[4,128,12,128]{3,1,2,0:T(8,128)(2,1)S(1)}, bf16[4,128,12,128]{3,1,2,0:T(8,128)(2,1)}, u32[]{:S(2)}, u32[]{:S(2)}) collective-permute-start(bf16[4,128,12,128]{3,1,2,0:T(8,128)(2,1)S(1)} %copy.204), channel_id=1, source_target_pairs={{0,2},{2,4},{4,6},{6,8},{8,10},{10,12},{12,14},{14,16},{16,18},{18... | collective-permute-start | bytes 4718600 | tf_op jit(solution)/shard_map/ppermute | solution.py:15
  603.4 7.2 %copy-start.25 = (bf16[8,128,12,128]{3,1,2,0:T(8,128)(2,1)S(1)}, bf16[8,128,12,128]{3,1,2,0:T(8,128)(2,1)}, u32[]{:S(2)}) copy-start(bf16[8,128,12,128]{3,1,2,0:T(8,128)(2,1)} %gather_fusion.5) | copy-start | bytes 9437188
  (68 other events, 242.4 us)
where the time goes:
time: 662 us; the launch traced here: 655 us
  waiting for transfers between devices  256 us (39%)
  local copies, waits for them, and re-layouts  169 us (26%)
  matrix products  92.9 us (14%)
  starting transfers between devices  72.6 us (11%)
  other arithmetic  40.5 us (6%)
  blocking collectives  22.8 us (3%)
    ppermute x20, waiting for transfers between devices, from_behind(): return lax.ppermute(block, axis, route)  227 us
    ppermute x20, starting transfers between devices, from_behind(): return lax.ppermute(block, axis, route)  60.6 us
    dot_general x11, matrix products, frame_partial(): jnp.einsum('bhqsk,bskhd->bqhd', probs.astype(jnp.bfloat16), picked_values...  52 us
    gather x14, local copies, waits for them, and re-layouts, frame_partial(): picked_keys = key_blocks[block_ids]  51.4 us
    gather x11, local copies, waits for them, and re-layouts, frame_partial(): picked_values = value_blocks[block_ids]  37.4 us
    dot_general x8, matrix products, frame_partial(): jnp.einsum('bqhd,bskhd->bhqsk', query_group, picked_keys, preferred_eleme...  27.8 us
    reduce_sum x7, other arithmetic, frame_partial(): part_sum = jnp.sum(probs, axis=(3, 4))  23.8 us
    all_to_all x1, blocking collectives, local(): lax.all_to_all(attended, 'head', split_axis=0, concat_axis=1, tiled=True)  22.8 us
  transfers between devices with their start and end apart: 23, of which 8 were waited for; matrix products, arithmetic and copies ran while one was open for 43% of the time, Pallas kernels for 0%

commit v1 on v0

--- a/solution.py
+++ b/solution.py
@@ -162,7 +162,10 @@
         state = merge_state(state, part)
     denominator = jnp.transpose(state[1], (0, 2, 1))[..., None]
     attended = (state[2] / denominator).reshape(frame_tokens, row_width).astype(jnp.bfloat16)
-    return lax.all_to_all(attended, "head", split_axis=0, concat_axis=1, tiled=True)
+    return jnp.concatenate(
+        lax.all_to_all(jnp.stack(jnp.split(attended, lax.axis_size("head"), axis=0)), "head", 0, 0),
+        axis=1,
+    )
 
 
 def solution(mesh):

time: 662 us -> 663 us (level)
  no operation moved by 1% of the time
where the time goes in v1:
time: 663 us; the launch traced here: 655 us
  waiting for transfers between devices  256 us (39%)
  local copies, waits for them, and re-layouts  169 us (25%)
  matrix products  92.9 us (14%)
  starting transfers between devices  72.6 us (11%)
  other arithmetic  40.7 us (6%)
  blocking collectives  22.7 us (3%)
    ppermute x20, waiting for transfers between devices, from_behind(): return lax.ppermute(block, axis, route)  227 us
    ppermute x20, starting transfers between devices, from_behind(): return lax.ppermute(block, axis, route)  60.6 us
    dot_general x11, matrix products, frame_partial(): jnp.einsum('bhqsk,bskhd->bqhd', probs.astype(jnp.bfloat16), picked_values...  52 us
    gather x14, local copies, waits for them, and re-layouts, frame_partial(): picked_keys = key_blocks[block_ids]  51.4 us
    gather x11, local copies, waits for them, and re-layouts, frame_partial(): picked_values = value_blocks[block_ids]  37.4 us
    dot_general x8, matrix products, frame_partial(): jnp.einsum('bqhd,bskhd->bhqsk', query_group, picked_keys, preferred_eleme...  27.8 us
    reduce_sum x7, other arithmetic, frame_partial(): part_sum = jnp.sum(probs, axis=(3, 4))  23.8 us
    all_to_all x1, blocking collectives, local(): lax.all_to_all(jnp.stack(jnp.split(attended, lax.axis_size('head'), axis=...  22.7 us
  transfers between devices with their start and end apart: 23, of which 8 were waited for; matrix products, arithmetic and copies ran while one was open for 43% of the time, Pallas kernels for 0%

profile of v1, /device:TPU:26, one launch (start us, length us, event | category | flops | bytes accessed | tf_op | source)
XLA Modules:
  0.0 655.3 jit_solution(5578897673872795329)
XLA Ops:
  9.6 16.3 %all-to-all-done.1 = bf16[256,2,1536]{0,2,1:T(8,128)(2,1)S(1)} async-done(((bf16[256,2,1536]{0,2,1:T(8,128)(2,1)}), bf16[256,2,1536]{0,2,1:T(8,128)(2,1)S(1)}, u32[]{:S(2)}, u32[]{:S(2)}) %all-to-all-start.1) | async-done | bytes 1572896 | tf_op jit(solution)/shard_map/all_to_all | solution.py:124
  35.6 12.6 %all-to-all-done.2 = bf16[256,2,1536]{0,2,1:T(8,128)(2,1)S(1)} async-done(((bf16[256,2,1536]{0,2,1:T(8,128)(2,1)}), bf16[256,2,1536]{0,2,1:T(8,128)(2,1)S(1)}, u32[]{:S(2)}, u32[]{:S(2)}) %all-to-all-start.2) | async-done | bytes 1572896 | tf_op jit(solution)/shard_map/all_to_all | solution.py:125
  48.2 4.6 all-to-all-start
  54.6 10.7 %copy.205 = bf16[2,256,1536]{1,0,2:T(2,128)(2,1)} copy(bf16[2,256,1536]{1,2,0:T(8,128)(2,1)S(1)} %bitcast.450) | data formatting | bytes 3145728 | tf_op jit(solution)/shard_map/all_to_all | solution.py:125
  65.3 5.2 reshape.380
  79.4 10.7 %copy.197 = bf16[2,256,1536]{1,0,2:T(2,128)(2,1)} copy(bf16[2,256,1536]{1,2,0:T(8,128)(2,1)S(1)} %bitcast.449) | data formatting | bytes 3145728 | tf_op jit(solution)/shard_map/convert_element_type | solution.py:133
  94.1 4.8 copy.190
  125.8 6.1 collective-permute-start.10
  140.1 5.5 gather_fusion
  152.3 4.3 copy.203
  157.5 5.6 fusion
  163.2 5.7 collective-permute-start.7
  170.2 9.8 %collective-permute-done.12 = bf16[4,128,12,128]{3,1,2,0:T(8,128)(2,1)} collective-permute-done((bf16[4,128,12,128]{3,1,2,0:T(8,128)(2,1)}, bf16[4,128,12,128]{3,1,2,0:T(8,128)(2,1)}, u32[]{:S(2)}, u32[]{:S(2)}) %collective-permute-start.12) | collective-permute-done | bytes 1572896 | tf_op jit(solution)/shard_map/ppermute | solution.py:15
  183.7 11.9 %bitcast_convert_fusion.2 = bf16[4,12,128,128]{3,2,1,0:T(8,128)(2,1)} fusion(f32[4,12,128,512]{2,3,1,0} %get-tuple-element.90, f32[4,12,128]{2,1,0:T(8,128)S(1)} %get-tuple-element.89, pred[4,4]{1,0:T(4,128)(4,1)S(1)} %copy-done.73, bf16[4,4,128,12,128]{4,2,3,1,0:T(8,128)(2,1)} %bitcast.448), kind=kOutput, calls=%fused_computation.84 | convolution fusion | flops 821821440 | bytes 20471824 | tf_op jit(solution)/shard_map/bhqsk,bskhd->bqhd/dot_general | solution.py:92
  195.5 12.1 %collective-permute-done.8 = bf16[4,128,12,128]{3,1,2,0:T(8,128)(2,1)} collective-permute-done((bf16[4,128,12,128]{3,1,2,0:T(8,128)(2,1)}, bf16[4,128,12,128]{3,1,2,0:T(8,128)(2,1)}, u32[]{:S(2)}, u32[]{:S(2)}) %collective-permute-start.8) | collective-permute-done | bytes 1572896 | tf_op jit(solution)/shard_map/ppermute | solution.py:15
  209.2 6.6 %fusion.1 = f32[4,12,128]{2,1,0:T(8,128)S(1)} fusion(f32[4,12,128,512]{2,3,1,0} %get-tuple-element.90, f32[4,12,128]{2,1,0:T(8,128)S(1)} %get-tuple-element.89, pred[4,4]{1,0:T(4,128)(4,1)S(1)} %copy-done.73), kind=kLoop, calls=%fused_computation.25 | loop fusion | flops 15722496 | bytes 12632080 | tf_op jit(solution)/shard_map/reduce_sum | solution.py:91
  236.3 48.9 %collective-permute-done.7 = bf16[4,128,12,128]{3,1,2,0:T(8,128)(2,1)} collective-permute-done((bf16[4,128,12,128]{3,1,2,0:T(8,128)(2,1)S(1)}, bf16[4,128,12,128]{3,1,2,0:T(8,128)(2,1)}, u32[]{:S(2)}, u32[]{:S(2)}) %collective-permute-start.7) | collective-permute-done | bytes 1572896 | tf_op jit(solution)/shard_map/ppermute | solution.py:15
  285.3 9.1 %collective-permute-start.19 = (bf16[4,128,12,128]{3,1,2,0:T(8,128)(2,1)S(1)}, bf16[4,128,12,128]{3,1,2,0:T(8,128)(2,1)}, u32[]{:S(2)}, u32[]{:S(2)}) collective-permute-start(bf16[4,128,12,128]{3,1,2,0:T(8,128)(2,1)S(1)} %copy.206), channel_id=1, source_target_pairs={{16,0},{18,2},{20,4},{22,6},{24,8},{26,10},{28,12},{30,14},{17,1},... | collective-permute-start | bytes 4718600 | tf_op jit(solution)/shard_map/ppermute | solution.py:15
  297.7 21.3 %collective-permute-done.6 = bf16[4,128,12,128]{3,1,2,0:T(8,128)(2,1)} collective-permute-done((bf16[4,128,12,128]{3,1,2,0:T(8,128)(2,1)}, bf16[4,128,12,128]{3,1,2,0:T(8,128)(2,1)}, u32[]{:S(2)}, u32[]{:S(2)}) %collective-permute-start.6) | collective-permute-done | bytes 1572896 | tf_op jit(solution)/shard_map/ppermute | solution.py:15
  319.1 7.5 %collective-permute-start.15 = (bf16[4,128,12,128]{3,1,2,0:T(8,128)(2,1)S(1)}, bf16[4,128,12,128]{3,1,2,0:T(8,128)(2,1)}, u32[]{:S(2)}, u32[]{:S(2)}) collective-permute-start(bf16[4,128,12,128]{3,1,2,0:T(8,128)(2,1)S(1)} %copy.206), channel_id=1, source_target_pairs={{8,0},{10,2},{12,4},{14,6},{16,8},{18,10},{20,12},{22,14},{24,16},... | collective-permute-start | bytes 4718600 | tf_op jit(solution)/shard_map/ppermute | solution.py:15
  341.8 4.4 fusion.56
  361.2 4.4 fusion.60
  373.7 52.1 %collective-permute-done.14 = bf16[4,128,12,128]{3,1,2,0:T(8,128)(2,1)} collective-permute-done((bf16[4,128,12,128]{3,1,2,0:T(8,128)(2,1)}, bf16[4,128,12,128]{3,1,2,0:T(8,128)(2,1)}, u32[]{:S(2)}, u32[]{:S(2)}) %collective-permute-start.14) | collective-permute-done | bytes 1572896 | tf_op jit(solution)/shard_map/ppermute | solution.py:15
  431.5 4.4 fusion.61
  476.1 5.2 fusion.13
  489.1 4.3 convolution_convert_fusion.2
  499.0 82.7 %collective-permute-done.17 = bf16[4,128,12,128]{3,1,2,0:T(8,128)(2,1)} collective-permute-done((bf16[4,128,12,128]{3,1,2,0:T(8,128)(2,1)S(1)}, bf16[4,128,12,128]{3,1,2,0:T(8,128)(2,1)}, u32[]{:S(2)}, u32[]{:S(2)}) %collective-permute-start.17) | collective-permute-done | bytes 1572896 | tf_op jit(solution)/shard_map/ppermute | solution.py:15
  584.1 4.3 convolution_convert_fusion.1
  599.4 4.1 gather_fusion.3
  603.5 7.2 %bitcast_convert_fusion.1 = bf16[4,12,128,128]{3,2,1,0:T(8,128)(2,1)} fusion(f32[4,12,128,256]{2,3,1,0} %get-tuple-element.88, f32[4,12,128]{2,1,0:T(8,128)S(1)} %get-tuple-element.87, pred[4,2]{1,0:T(4,128)(4,1)S(1)} %copy-done.54, bf16[4,2,128,12,128]{4,2,3,1,0:T(8,128)(2,1)} %bitcast.455), kind=kOutput, calls=%fused_computation.79 | convolution fusion | flops 411303936 | bytes 11034632 | tf_op jit(solution)/shard_map/bhqsk,bskhd->bqhd/dot_general | solution.py:92
  617.8 9.7 %fusion.23 = bf16[4,128,12,128]{1,3,2,0:T(8,128)(2,1)S(1)} fusion(bf16[4,12,128,128]{3,2,1,0:T(8,128)(2,1)} %convolution_convert_fusion.1, bf16[4,12,128,128]{3,2,1,0:T(8,128)(2,1)} %convolution_convert_fusion.2, bf16[4,12,128,128]{3,2,1,0:T(8,128)(2,1)} %convolution_convert_fusion.3, bf16[4,12,128,128]{3,2,1,0:T(8,128)(2,1)} %convolution_convert_fusion.4, ...), kind=kOutput, calls=%fused_computation.49 | convolution fusion | flops 241434624 | bytes 22609924 | tf_op jit(solution)/shard_map/bhqsk,bskhd->bqhd/dot_general | solution.py:92
  630.4 22.7 %all_to_all.47 = bf16[2,256,1536]{1,2,0:T(8,128)(2,1)S(1)} all-to-all(bf16[2,256,1536]{1,2,0:T(8,128)(2,1)S(1)} %pad_maximum_fusion.2), channel_id=1, replica_groups=mesh['seq'=16,'head'=2] {'head'}, dimensions={0} | all-to-all | bytes 3145728 | tf_op jit(solution)/shard_map/all_to_all | solution.py:166
  (303 shorter events, 229.0 us)
Async XLA Ops:
  0.0 7.4 %copy-start.31 = (bf16[256,3072]{1,0:T(8,128)(2,1)S(1)}, bf16[256,3072]{1,0:T(8,128)(2,1)}, u32[]{:S(2)}) copy-start(bf16[256,3072]{1,0:T(8,128)(2,1)} %param.7) | copy-start | bytes 4718596
  2.7 23.2 %all-to-all-start.1 = ((bf16[256,2,1536]{0,2,1:T(8,128)(2,1)}), bf16[256,2,1536]{0,2,1:T(8,128)(2,1)S(1)}, u32[]{:S(2)}, u32[]{:S(2)}) async-start(bf16[256,2,1536]{0,2,1:T(8,128)(2,1)} %bitcast.3), calls=%async_computation.1 | async-start | bytes 3145728 | tf_op jit(solution)/shard_map/all_to_all | solution.py:124
  25.9 22.3 %all-to-all-start.2 = ((bf16[256,2,1536]{0,2,1:T(8,128)(2,1)}), bf16[256,2,1536]{0,2,1:T(8,128)(2,1)S(1)}, u32[]{:S(2)}, u32[]{:S(2)}) async-start(bf16[256,2,1536]{0,2,1:T(8,128)(2,1)} %bitcast.451), calls=%async_computation.2 | async-start | bytes 3145728 | tf_op jit(solution)/shard_map/all_to_all | solution.py:125
  48.2 46.0 %all-to-all-start = ((bf16[256,2,1536]{0,2,1:T(8,128)(2,1)}), bf16[256,2,1536]{0,2,1:T(8,128)(2,1)}, u32[]{:S(2)}, u32[]{:S(2)}) async-start(bf16[256,2,1536]{0,2,1:T(8,128)(2,1)} %bitcast.452), calls=%async_computation | async-start | bytes 3145728 | tf_op jit(solution)/shard_map/all_to_all | solution.py:122
  73.2 61.4 %collective-permute-start.13 = (bf16[4,128,12,128]{3,1,2,0:T(8,128)(2,1)S(1)}, bf16[4,128,12,128]{3,1,2,0:T(8,128)(2,1)}, u32[]{:S(2)}, u32[]{:S(2)}) collective-permute-start(bf16[4,128,12,128]{3,1,2,0:T(8,128)(2,1)S(1)} %copy.206), channel_id=1, source_target_pairs={{0,8},{2,10},{4,12},{6,14},{8,16},{10,18},{12,20},{14,22},{16,24},... | collective-permute-start | bytes 4718600 | tf_op jit(solution)/shard_map/ppermute | solution.py:15
  74.5 88.7 %collective-permute-start.11 = (bf16[4,128,12,128]{3,1,2,0:T(8,128)(2,1)S(1)}, bf16[4,128,12,128]{3,1,2,0:T(8,128)(2,1)}, u32[]{:S(2)}, u32[]{:S(2)}) collective-permute-start(bf16[4,128,12,128]{3,1,2,0:T(8,128)(2,1)S(1)} %copy.206), channel_id=1, source_target_pairs={{6,0},{8,2},{10,4},{12,6},{14,8},{16,10},{18,12},{20,14},{22,16},{... | collective-permute-start | bytes 4718600 | tf_op jit(solution)/shard_map/ppermute | solution.py:15
  77.6 91.3 %collective-permute-start.9 = (bf16[4,128,12,128]{3,1,2,0:T(8,128)(2,1)S(1)}, bf16[4,128,12,128]{3,1,2,0:T(8,128)(2,1)}, u32[]{:S(2)}, u32[]{:S(2)}) collective-permute-start(bf16[4,128,12,128]{3,1,2,0:T(8,128)(2,1)S(1)} %copy.206), channel_id=1, source_target_pairs={{0,6},{2,8},{4,10},{6,12},{8,14},{10,16},{12,18},{14,20},{16,22},{... | collective-permute-start | bytes 4718600 | tf_op jit(solution)/shard_map/ppermute | solution.py:15
  101.7 34.4 %copy-start.22 = (bf16[512,12,128]{0,2,1:T(8,128)(2,1)}, bf16[512,12,128]{0,2,1:T(8,128)(2,1)S(1)}, u32[]{:S(2)}) copy-start(bf16[512,12,128]{0,2,1:T(8,128)(2,1)S(1)} %convert_element_type.181) | copy-start | bytes 4718596
  119.0 13.6 %copy-start.74 = (s32[4,1]{0,1:T(1,128)S(1)}, s32[4,1]{0,1:T(1,128)}, u32[]{:S(2)}) copy-start(s32[4,1]{0,1:T(1,128)} %copy.291) | copy-start | bytes 52
  119.0 17.0 %copy-start.32 = (bf16[512,12,8,1]{0,2,3,1:T(8,128)(2,1)S(1)}, bf16[512,12,8,1]{0,2,3,1:T(8,128)(2,1)}, u32[]{:S(2)}) copy-start(bf16[512,12,8,1]{0,2,3,1:T(8,128)(2,1)} %get-tuple-element.69) | copy-start | bytes 294916
  119.0 17.0 %copy-start.33 = (bf16[512,12,8,1]{0,2,3,1:T(8,128)(2,1)S(1)}, bf16[512,12,8,1]{0,2,3,1:T(8,128)(2,1)}, u32[]{:S(2)}) copy-start(bf16[512,12,8,1]{0,2,3,1:T(8,128)(2,1)} %get-tuple-element.70) | copy-start | bytes 294916
  120.6 11.3 %copy-start.72 = (s32[64,16]{0,1:T(8,128)S(1)}, s32[64,16]{0,1:T(8,128)}, u32[]{:S(2)}) copy-start(s32[64,16]{0,1:T(8,128)} %param.9) | copy-start | bytes 12292
  120.6 11.4 %copy-start.75 = (s32[4,1]{0,1:T(1,128)S(1)}, s32[4,1]{0,1:T(1,128)}, u32[]{:S(2)}) copy-start(s32[4,1]{0,1:T(1,128)} %copy.290) | copy-start | bytes 52
  124.5 55.4 %collective-permute-start.12 = (bf16[4,128,12,128]{3,1,2,0:T(8,128)(2,1)}, bf16[4,128,12,128]{3,1,2,0:T(8,128)(2,1)}, u32[]{:S(2)}, u32[]{:S(2)}) collective-permute-start(bf16[4,128,12,128]{3,1,2,0:T(8,128)(2,1)} %pad_maximum_fusion.1), channel_id=1, source_target_pairs={{0,8},{2,10},{4,12},{6,14},{8,16},{10,18},{12,20},{14,22},{16,24},... | collective-permute-start | bytes 4718600 | tf_op jit(solution)/shard_map/ppermute | solution.py:15
  125.8 56.6 %collective-permute-start.10 = (bf16[4,128,12,128]{3,1,2,0:T(8,128)(2,1)}, bf16[4,128,12,128]{3,1,2,0:T(8,128)(2,1)}, u32[]{:S(2)}, u32[]{:S(2)}) collective-permute-start(bf16[4,128,12,128]{3,1,2,0:T(8,128)(2,1)} %pad_maximum_fusion.1), channel_id=1, source_target_pairs={{6,0},{8,2},{10,4},{12,6},{14,8},{16,10},{18,12},{20,14},{22,16},{... | collective-permute-start | bytes 4718600 | tf_op jit(solution)/shard_map/ppermute | solution.py:15
  134.6 73.1 %collective-permute-start.8 = (bf16[4,128,12,128]{3,1,2,0:T(8,128)(2,1)}, bf16[4,128,12,128]{3,1,2,0:T(8,128)(2,1)}, u32[]{:S(2)}, u32[]{:S(2)}) collective-permute-start(bf16[4,128,12,128]{3,1,2,0:T(8,128)(2,1)} %pad_maximum_fusion.1), channel_id=1, source_target_pairs={{0,6},{2,8},{4,10},{6,12},{8,14},{10,16},{12,18},{14,20},{16,22},{... | collective-permute-start | bytes 4718600 | tf_op jit(solution)/shard_map/ppermute | solution.py:15
  163.2 122.1 %collective-permute-start.7 = (bf16[4,128,12,128]{3,1,2,0:T(8,128)(2,1)S(1)}, bf16[4,128,12,128]{3,1,2,0:T(8,128)(2,1)}, u32[]{:S(2)}, u32[]{:S(2)}) collective-permute-start(bf16[4,128,12,128]{3,1,2,0:T(8,128)(2,1)S(1)} %copy.206), channel_id=1, source_target_pairs={{4,0},{6,2},{8,4},{10,6},{12,8},{14,10},{16,12},{18,14},{20,16},{2... | collective-permute-start | bytes 4718600 | tf_op jit(solution)/shard_map/ppermute | solution.py:15
  168.9 161.1 %collective-permute-start.5 = (bf16[4,128,12,128]{3,1,2,0:T(8,128)(2,1)S(1)}, bf16[4,128,12,128]{3,1,2,0:T(8,128)(2,1)}, u32[]{:S(2)}, u32[]{:S(2)}) collective-permute-start(bf16[4,128,12,128]{3,1,2,0:T(8,128)(2,1)S(1)} %copy.206), channel_id=1, source_target_pairs={{0,4},{2,6},{4,8},{6,10},{8,12},{10,14},{12,16},{14,18},{16,20},{1... | collective-permute-start | bytes 4718600 | tf_op jit(solution)/shard_map/ppermute | solution.py:15
  180.0 139.1 %collective-permute-start.6 = (bf16[4,128,12,128]{3,1,2,0:T(8,128)(2,1)}, bf16[4,128,12,128]{3,1,2,0:T(8,128)(2,1)}, u32[]{:S(2)}, u32[]{:S(2)}) collective-permute-start(bf16[4,128,12,128]{3,1,2,0:T(8,128)(2,1)} %pad_maximum_fusion.1), channel_id=1, source_target_pairs={{4,0},{6,2},{8,4},{10,6},{12,8},{14,10},{16,12},{18,14},{20,16},{2... | collective-permute-start | bytes 4718600 | tf_op jit(solution)/shard_map/ppermute | solution.py:15
  182.4 153.5 %collective-permute-start.4 = (bf16[4,128,12,128]{3,1,2,0:T(8,128)(2,1)}, bf16[4,128,12,128]{3,1,2,0:T(8,128)(2,1)}, u32[]{:S(2)}, u32[]{:S(2)}) collective-permute-start(bf16[4,128,12,128]{3,1,2,0:T(8,128)(2,1)} %pad_maximum_fusion.1), channel_id=1, source_target_pairs={{0,4},{2,6},{4,8},{6,10},{8,12},{10,14},{12,16},{14,18},{16,20},{1... | collective-permute-start | bytes 4718600 | tf_op jit(solution)/shard_map/ppermute | solution.py:15
  207.7 147.4 %collective-permute-start.16 = (bf16[4,128,12,128]{3,1,2,0:T(8,128)(2,1)}, bf16[4,128,12,128]{3,1,2,0:T(8,128)(2,1)}, u32[]{:S(2)}, u32[]{:S(2)}) collective-permute-start(bf16[4,128,12,128]{3,1,2,0:T(8,128)(2,1)} %pad_maximum_fusion.1), channel_id=1, source_target_pairs={{0,16},{2,18},{4,20},{6,22},{8,24},{10,26},{12,28},{14,30},{1,17},... | collective-permute-start | bytes 4718600 | tf_op jit(solution)/shard_map/ppermute | solution.py:15
  285.3 328.9 %collective-permute-start.19 = (bf16[4,128,12,128]{3,1,2,0:T(8,128)(2,1)S(1)}, bf16[4,128,12,128]{3,1,2,0:T(8,128)(2,1)}, u32[]{:S(2)}, u32[]{:S(2)}) collective-permute-start(bf16[4,128,12,128]{3,1,2,0:T(8,128)(2,1)S(1)} %copy.206), channel_id=1, source_target_pairs={{16,0},{18,2},{20,4},{22,6},{24,8},{26,10},{28,12},{30,14},{17,1},... | collective-permute-start | bytes 4718600 | tf_op jit(solution)/shard_map/ppermute | solution.py:15
  319.1 167.6 %collective-permute-start.15 = (bf16[4,128,12,128]{3,1,2,0:T(8,128)(2,1)S(1)}, bf16[4,128,12,128]{3,1,2,0:T(8,128)(2,1)}, u32[]{:S(2)}, u32[]{:S(2)}) collective-permute-start(bf16[4,128,12,128]{3,1,2,0:T(8,128)(2,1)S(1)} %copy.206), channel_id=1, source_target_pairs={{8,0},{10,2},{12,4},{14,6},{16,8},{18,10},{20,12},{22,14},{24,16},... | collective-permute-start | bytes 4718600 | tf_op jit(solution)/shard_map/ppermute | solution.py:15
  330.0 140.7 %collective-permute-start.18 = (bf16[4,128,12,128]{3,1,2,0:T(8,128)(2,1)}, bf16[4,128,12,128]{3,1,2,0:T(8,128)(2,1)}, u32[]{:S(2)}, u32[]{:S(2)}) collective-permute-start(bf16[4,128,12,128]{3,1,2,0:T(8,128)(2,1)} %pad_maximum_fusion.1), channel_id=1, source_target_pairs={{16,0},{18,2},{20,4},{22,6},{24,8},{26,10},{28,12},{30,14},{17,1},... | collective-permute-start | bytes 4718600 | tf_op jit(solution)/shard_map/ppermute | solution.py:15
  335.9 89.8 %collective-permute-start.14 = (bf16[4,128,12,128]{3,1,2,0:T(8,128)(2,1)}, bf16[4,128,12,128]{3,1,2,0:T(8,128)(2,1)}, u32[]{:S(2)}, u32[]{:S(2)}) collective-permute-start(bf16[4,128,12,128]{3,1,2,0:T(8,128)(2,1)} %pad_maximum_fusion.1), channel_id=1, source_target_pairs={{8,0},{10,2},{12,4},{14,6},{16,8},{18,10},{20,12},{22,14},{24,16},... | collective-permute-start | bytes 4718600 | tf_op jit(solution)/shard_map/ppermute | solution.py:15
  355.1 88.9 %collective-permute-start.2 = (bf16[4,128,12,128]{3,1,2,0:T(8,128)(2,1)}, bf16[4,128,12,128]{3,1,2,0:T(8,128)(2,1)}, u32[]{:S(2)}, u32[]{:S(2)}) collective-permute-start(bf16[4,128,12,128]{3,1,2,0:T(8,128)(2,1)} %pad_maximum_fusion.1), channel_id=1, source_target_pairs={{2,0},{4,2},{6,4},{8,6},{10,8},{12,10},{14,12},{16,14},{18,16},{20... | collective-permute-start | bytes 4718600 | tf_op jit(solution)/shard_map/ppermute | solution.py:15
  373.7 57.8 %copy-start.60 = (pred[4]{0:T(512)(128)(4,1)S(1)}, pred[4]{0:T(512)(128)(4,1)}, u32[]{:S(2)}) copy-start(pred[4]{0:T(512)(128)(4,1)} %get-tuple-element.59) | copy-start | bytes 16
  425.7 27.6 %collective-permute-start = (bf16[4,128,12,128]{3,1,2,0:T(8,128)(2,1)}, bf16[4,128,12,128]{3,1,2,0:T(8,128)(2,1)}, u32[]{:S(2)}, u32[]{:S(2)}) collective-permute-start(bf16[4,128,12,128]{3,1,2,0:T(8,128)(2,1)} %pad_maximum_fusion.1), channel_id=1, source_target_pairs={{0,2},{2,4},{4,6},{6,8},{8,10},{10,12},{12,14},{14,16},{16,18},{18... | collective-permute-start | bytes 4718600 | tf_op jit(solution)/shard_map/ppermute | solution.py:15
  444.0 137.6 %collective-permute-start.17 = (bf16[4,128,12,128]{3,1,2,0:T(8,128)(2,1)S(1)}, bf16[4,128,12,128]{3,1,2,0:T(8,128)(2,1)}, u32[]{:S(2)}, u32[]{:S(2)}) collective-permute-start(bf16[4,128,12,128]{3,1,2,0:T(8,128)(2,1)S(1)} %copy.206), channel_id=1, source_target_pairs={{0,16},{2,18},{4,20},{6,22},{8,24},{10,26},{12,28},{14,30},{1,17},... | collective-permute-start | bytes 4718600 | tf_op jit(solution)/shard_map/ppermute | solution.py:15
  453.3 142.1 %collective-permute-start.3 = (bf16[4,128,12,128]{3,1,2,0:T(8,128)(2,1)S(1)}, bf16[4,128,12,128]{3,1,2,0:T(8,128)(2,1)}, u32[]{:S(2)}, u32[]{:S(2)}) collective-permute-start(bf16[4,128,12,128]{3,1,2,0:T(8,128)(2,1)S(1)} %copy.206), channel_id=1, source_target_pairs={{2,0},{4,2},{6,4},{8,6},{10,8},{12,10},{14,12},{16,14},{18,16},{20... | collective-permute-start | bytes 4718600 | tf_op jit(solution)/shard_map/ppermute | solution.py:15
  470.7 128.7 %collective-permute-start.1 = (bf16[4,128,12,128]{3,1,2,0:T(8,128)(2,1)S(1)}, bf16[4,128,12,128]{3,1,2,0:T(8,128)(2,1)}, u32[]{:S(2)}, u32[]{:S(2)}) collective-permute-start(bf16[4,128,12,128]{3,1,2,0:T(8,128)(2,1)S(1)} %copy.206), channel_id=1, source_target_pairs={{0,2},{2,4},{4,6},{6,8},{8,10},{10,12},{12,14},{14,16},{16,18},{18... | collective-permute-start | bytes 4718600 | tf_op jit(solution)/shard_map/ppermute | solution.py:15
  603.5 7.2 %copy-start.25 = (bf16[8,128,12,128]{3,1,2,0:T(8,128)(2,1)S(1)}, bf16[8,128,12,128]{3,1,2,0:T(8,128)(2,1)}, u32[]{:S(2)}) copy-start(bf16[8,128,12,128]{3,1,2,0:T(8,128)(2,1)} %gather_fusion.5) | copy-start | bytes 9437188
  (68 other events, 242.6 us)
